TPU v7x, 256 devices: a whole 4x4x8 slice. The times are simulated.
256 devices in a mesh: blk: 32 (over z, x_lo, core), head: 8 (over x_hi, y).
Axes of the slice: x: 4 (x_hi: 2, x_lo: 2; x = x_hi * 2 + x_lo), y: 4, z: 8, core: 2. Of those that a mesh axis runs over, the one named last changes fastest.
Arguments:
- query_tokens: bfloat16 [16384, 3072], P(('blk', 'head')), may hold values from -12 to 12
- key_tokens: bfloat16 [16384, 3072], P(('blk', 'head')), may hold values from -6 to 6
- value_tokens: bfloat16 [16384, 3072], P(('blk', 'head')), may hold values from -6 to 6
- out_weight: bfloat16 [3072, 3072], P('head'), may hold values from -1.75 to 1.75
- kv_blocks: int32 [128, 16], P('blk'), may hold values from -1 to 127, as said below
Outputs:
- projected: bfloat16 [16384, 3072], P(('blk', 'head'))
Inputs may be any that keep to these rules, and one draw needn't show every extreme that they name: `kv_blocks`: row i lists the key blocks of 128 tokens that query block i attends to; let G = floor(i / 4). Entry 0 is i. Entry 1 is one of the blocks 4 * M to 4 * M + 3 with M = (G + 16) mod 32. Entry j >= 2 is -1 (absent) or one of the blocks 4 * (G + o) to 4 * (G + o) + 3, with o = j // 2 for even j and o = -(j - 1) // 2 for odd j; it is present whenever j < 8 and those blocks exist. Entries of one row are distinct.
All inputs are finite; a program needn't handle non-finite values.
Results may differ from a plain program's by a relative error of at most 0.012.
Values may be sent and summed in bfloat16 or wider, within the bound.
A program may use at most 128 MiB of HBM per device.

v0:
```python
import math
import jax
import jax.numpy as jnp
from jax import lax
from jax.sharding import PartitionSpec as P

HD = 128
masked_low = -1e30


def sparse_attend(query_sets, key_sets, value_sets, present):
    blocks_dev = present.shape[0]
    slots = present.shape[1]
    block_rows = query_sets.shape[2]
    scaling = 1.0 / math.sqrt(HD)
    allowed = jnp.broadcast_to(present[:, :, None], (blocks_dev, slots, block_rows)).reshape(
        blocks_dev, slots * block_rows
    )
    scores = (
        jnp.einsum("hbqd,hbkd->hbqk", query_sets, key_sets, preferred_element_type=jnp.float32)
        * scaling
    )
    mask_full = allowed[None, :, None, :]
    peak_value = jnp.max(jnp.where(mask_full, scores, masked_low), axis=-1, keepdims=True)
    weights = jnp.where(mask_full, jnp.exp(scores - peak_value), 0.0)
    denom = jnp.sum(weights, axis=-1)
    outputs = jnp.einsum(
        "hbqk,hbkd->hbqd",
        weights.astype(jnp.bfloat16),
        value_sets,
        preferred_element_type=jnp.float32,
    )
    return outputs / denom[..., None]


def on_device(query_tokens, key_tokens, value_tokens, out_weight, kv_blocks):
    queries, key_rows, value_rows = (
        lax.all_to_all(query_tokens, "head", split_axis=1, concat_axis=0, tiled=True),
        lax.all_to_all(key_tokens, "head", split_axis=1, concat_axis=0, tiled=True),
        lax.all_to_all(value_tokens, "head", split_axis=1, concat_axis=0, tiled=True),
    )
    row_total = queries.shape[0]
    feature_width = queries.shape[1]
    heads_dev = feature_width // HD
    blocks_dev = kv_blocks.shape[0]
    block_rows = row_total // blocks_dev
    slots = kv_blocks.shape[1]
    query_heads = queries.reshape(row_total, heads_dev, HD).transpose(1, 0, 2)
    query_sets = query_heads.reshape(heads_dev, blocks_dev, block_rows, HD)
    key_heads = key_rows.reshape(row_total, heads_dev, HD).transpose(1, 0, 2)
    value_heads = value_rows.reshape(row_total, heads_dev, HD).transpose(1, 0, 2)
    present = kv_blocks >= 0
    safe_index = jnp.maximum(kv_blocks, 0)
    gathered_keys, gathered_values = (
        lax.all_gather(key_heads, "blk", axis=1, tiled=True),
        lax.all_gather(value_heads, "blk", axis=1, tiled=True),
    )
    total_blocks = gathered_keys.shape[1] // block_rows
    source_keys = gathered_keys.reshape(heads_dev, total_blocks, block_rows, HD)
    source_values = gathered_values.reshape(heads_dev, total_blocks, block_rows, HD)
    flat_index = safe_index.reshape(blocks_dev * slots)
    key_sets = jnp.take(source_keys, flat_index, axis=1).reshape(
        heads_dev, blocks_dev, slots * block_rows, HD
    )
    value_sets = jnp.take(source_values, flat_index, axis=1).reshape(
        heads_dev, blocks_dev, slots * block_rows, HD
    )
    outputs = sparse_attend(query_sets, key_sets, value_sets, present)
    attended = (
        outputs.reshape(heads_dev, row_total, HD)
        .transpose(1, 0, 2)
        .reshape(row_total, feature_width)
    )
    attended = attended.astype(jnp.bfloat16)
    return lax.psum_scatter(
        jnp.dot(attended, out_weight, preferred_element_type=jnp.float32).astype(jnp.bfloat16),
        "head",
        scatter_dimension=0,
        tiled=True,
    )


def solution(mesh):
    placed = (
        P(("blk", "head"), None),
        P(("blk", "head"), None),
        P(("blk", "head"), None),
        P("head", None),
        P("blk", None),
    )
    return jax.shard_map(
        on_device, mesh=mesh, in_specs=placed, out_specs=P(("blk", "head"), None), check_vma=False
    )
```

profile of v0, /device:TPU:32, one launch (start us, length us, event | category | flops | bytes accessed | tf_op | source)
XLA Modules:
  0.0 322.1 jit_solution(16858350131159604797)
XLA Ops:
  6.5 0.0 copy-start
  6.5 0.0 copy-start.1
  6.5 0.0 all-gather.3.cloned.1.call-start
  6.5 1.2 copy.46
  7.7 16.9 %all_to_all.48 = bf16[64,8,384]{2,0,1:T(8,128)(2,1)S(1)} all-to-all(bf16[64,8,384]{2,0,1:T(8,128)(2,1)S(1)} %bitcast.64), channel_id=1, replica_groups=mesh['blk'=32,'head'=8] {'head'}, dimensions={1} | all-to-all | bytes 786432 | tf_op jit(solution)/shard_map/all_to_all | solution.py:39
  24.7 0.1 reshape.52
  24.8 0.8 copy.26
  25.6 0.0 all-gather.3.cloned.1.call-update
  25.6 0.0 all-gather.5.cloned.1.call-start
  25.6 1.0 copy.44
  26.7 12.0 %all_to_all.49 = bf16[64,8,384]{2,0,1:T(8,128)(2,1)S(1)} all-to-all(bf16[64,8,384]{2,0,1:T(8,128)(2,1)S(1)} %bitcast.65), channel_id=1, replica_groups=mesh['blk'=32,'head'=8] {'head'}, dimensions={1} | all-to-all | bytes 786432 | tf_op jit(solution)/shard_map/all_to_all | solution.py:40
  38.7 0.1 reshape.58
  38.8 0.8 copy.31
  39.7 0.0 all-gather.5.cloned.1.call-update
  39.7 1.9 copy.45
  41.5 3.5 %all-to-all-start.1 = ((bf16[64,8,384]{2,0,1:T(8,128)(2,1)}), bf16[64,8,384]{2,0,1:T(8,128)(2,1)S(1)}, u32[]{:S(2)}, u32[]{:S(2)}) async-start(bf16[64,8,384]{2,0,1:T(8,128)(2,1)} %bitcast.51), calls=%async_computation.1 | async-start | bytes 786432 | tf_op jit(solution)/shard_map/all_to_all | solution.py:38
  45.0 0.0 reduce-scatter.2.cloned.1.call-start
  45.1 0.0 copy-done.1
  45.1 0.1 reshape.54
  45.2 0.1 broadcast_bitcast_fusion
  45.3 8.9 %all-to-all-done.1 = bf16[64,8,384]{2,0,1:T(8,128)(2,1)S(1)} async-done(((bf16[64,8,384]{2,0,1:T(8,128)(2,1)}), bf16[64,8,384]{2,0,1:T(8,128)(2,1)S(1)}, u32[]{:S(2)}, u32[]{:S(2)}) %all-to-all-start.1) | async-done | bytes 393248 | tf_op jit(solution)/shard_map/all_to_all | solution.py:38
  54.2 0.1 reshape.56
  54.3 0.1 copy.29
  54.4 51.7 %all-gather.3.cloned.1.call-done = bf16[3,16384,128]{2,1,0:T(8,128)(2,1)} async-done(((bf16[3,512,128]{2,1,0:T(8,128)(2,1)}), bf16[3,16384,128]{2,1,0:T(8,128)(2,1)}) %all-gather.3.cloned.1.call-update) | async-done | bytes 12582928 | tf_op jit(solution)/shard_map/all_gather | solution.py:55
  106.1 8.6 %gather_fusion = bf16[64,3,128,128]{3,2,1,0:T(8,128)(2,1)} fusion(bf16[3,128,128,128]{3,2,1,0:T(8,128)(2,1)} %bitcast.56, s32[1024]{0:T(1024)S(1)} %pad_clamp_fusion), kind=kCustom, calls=%fused_computation.clone | custom fusion | bytes 12583168 | tf_op jit(solution)/shard_map/jit(_take)/gather | solution.py:62
  114.7 72.9 %all-gather.5.cloned.1.call-done = bf16[3,16384,128]{2,1,0:T(8,128)(2,1)} async-done(((bf16[3,512,128]{2,1,0:T(8,128)(2,1)}), bf16[3,16384,128]{2,1,0:T(8,128)(2,1)}) %all-gather.5.cloned.1.call-update) | async-done | bytes 12582928 | tf_op jit(solution)/shard_map/all_gather | solution.py:56
  187.6 8.5 %gather_fusion.1 = bf16[64,3,128,128]{3,2,1,0:T(8,128)(2,1)} fusion(bf16[3,128,128,128]{3,2,1,0:T(8,128)(2,1)} %bitcast.57, s32[1024]{0:T(1024)S(1)} %pad_clamp_fusion), kind=kCustom, calls=%fused_computation.1.clone | custom fusion | bytes 12583168 | tf_op jit(solution)/shard_map/jit(_take)/gather | solution.py:65
  196.1 5.5 %select_bitcast_fusion.1 = (bf16[3,64,128,128]{3,2,0,1:T(8,128)(2,1)S(1)}, bf16[3,64,128,128]{3,2,0,1:T(8,128)(2,1)S(1)}) fusion(bf16[64,3,128,128]{3,2,1,0:T(8,128)(2,1)} %gather_fusion, pred[64]{0:T(512)(128)(4,1)S(1)} %compare_and_fusion, bf16[64,3,128,128]{3,2,1,0:T(8,128)(2,1)} %gather_fusion.1), kind=kLoop, calls=%fused_computation.11 | loop fusion | flops 6291456 | bytes 25165888 | tf_op jit(solution)/shard_map/jit(_take)/select_n | solution.py:62
  201.7 4.0 %copy.27 = bf16[3,64,128,128]{3,2,1,0:T(8,128)(2,1)} copy(bf16[3,64,128,128]{3,2,0,1:T(8,128)(2,1)S(1)} %get-tuple-element.6) | data formatting | bytes 12582912 | tf_op jit(solution)/shard_map/jit(_take)/select_n | solution.py:62
  205.7 4.0 %copy.32 = bf16[3,64,128,128]{3,2,1,0:T(8,128)(2,1)} copy(bf16[3,64,128,128]{3,2,0,1:T(8,128)(2,1)S(1)} %get-tuple-element.7) | data formatting | bytes 12582912 | tf_op jit(solution)/shard_map/jit(_take)/select_n | solution.py:65
  209.7 10.3 %bitcast_reduce_fusion = (f32[3,4,128]{2,1,0:T(4,128)S(1)}, bf16[3,4,2048,128]{3,2,1,0:T(8,128)(2,1)}) fusion(pred[4,2048]{1,0:T(4,128)(4,1)S(1)} %bitcast.72, bf16[3,4,2048,128]{3,2,1,0:T(8,128)(2,1)} %bitcast.54, bf16[3,4,128,128]{3,2,1,0:T(8,128)(2,1)S(1)} %bitcast.66), kind=kOutput, calls=%fused_computation.3 | convolution fusion | flops 1632634880 | bytes 12990464 | tf_op jit(solution)/shard_map/sub | solution.py:25
  220.0 6.6 %fusion.10 = bf16[3,4,128,128]{3,2,1,0:T(8,128)(2,1)S(1)} fusion(bf16[3,4,2048,128]{3,2,1,0:T(8,128)(2,1)} %bitcast.55, f32[3,4,128]{2,1,0:T(4,128)S(1)} %get-tuple-element.8, bf16[3,4,2048,128]{3,2,1,0:T(8,128)(2,1)} %get-tuple-element.9), kind=kOutput, calls=%fused_computation.17 | convolution fusion | flops 805699584 | bytes 12982272 | tf_op jit(solution)/shard_map/hbqk,hbkd->hbqd/dot_general | solution.py:27
  226.7 0.2 copy.34
  226.9 0.0 copy-done
  226.9 3.5 %convolution_convert_fusion = bf16[512,3072]{1,0:T(8,128)(2,1)} fusion(bf16[512,384]{0,1:T(8,128)(2,1)S(1)} %bitcast.71, bf16[384,3072]{1,0:T(8,128)(2,1)S(1)} %copy-done), kind=kOutput, calls=%fused_computation.15 | convolution fusion | flops 1209532416 | bytes 5898240 | tf_op jit(solution)/shard_map/dot_general | solution.py:76
  230.3 0.0 reduce-scatter.2.cloned.1.call-update
  230.4 85.2 %reduce-scatter.2.cloned.1.call-done = bf16[64,3072]{1,0:T(8,128)(2,1)} async-done(((bf16[512,3072]{1,0:T(8,128)(2,1)}), bf16[64,3072]{1,0:T(8,128)(2,1)}) %reduce-scatter.2.cloned.1.call-update) | async-done | bytes 393232 | tf_op jit(solution)/shard_map/reduce_scatter | solution.py:75
  (6 shorter events, 0.0 us)
Async XLA Ops:
  6.5 220.3 %copy-start = (bf16[384,3072]{1,0:T(8,128)(2,1)S(1)}, bf16[384,3072]{1,0:T(8,128)(2,1)}, u32[]{:S(2)}) copy-start(bf16[384,3072]{1,0:T(8,128)(2,1)} %param.10) | copy-start | bytes 7077892
  6.5 38.5 %copy-start.1 = (s32[4,16]{1,0:T(4,128)S(1)}, s32[4,16]{1,0:T(4,128)}, u32[]{:S(2)}) copy-start(s32[4,16]{1,0:T(4,128)} %param.11) | copy-start | bytes 772
  6.5 99.5 %all-gather.3.cloned.1.call-start = ((), (), s32[]{:S(2)}) async-start(), calls=%async_computation.4 | async-start | bytes 12976128 | tf_op jit(solution)/shard_map/all_gather | solution.py:55
  25.6 162.0 %all-gather.5.cloned.1.call-start = ((), (), s32[]{:S(2)}) async-start(), calls=%async_computation.5 | async-start | bytes 12976128 | tf_op jit(solution)/shard_map/all_gather | solution.py:56
  41.5 12.6 %all-to-all-start.1 = ((bf16[64,8,384]{2,0,1:T(8,128)(2,1)}), bf16[64,8,384]{2,0,1:T(8,128)(2,1)S(1)}, u32[]{:S(2)}, u32[]{:S(2)}) async-start(bf16[64,8,384]{2,0,1:T(8,128)(2,1)} %bitcast.51), calls=%async_computation.1 | async-start | bytes 786432 | tf_op jit(solution)/shard_map/all_to_all | solution.py:38
  45.0 270.6 %reduce-scatter.2.cloned.1.call-start = ((), (), s32[]{:S(2)}) async-start(), calls=%async_computation.6 | async-start | bytes 3538944 | tf_op jit(solution)/shard_map/reduce_scatter | solution.py:75
Sparse Core Ops, SparseCore 0:
  25.7 80.2 all-gather.2
  107.9 79.6 all-gather.4
  230.5 85.0 reduce-scatter.1
where the time goes:
time: 323 us; the launch traced here: 322 us
  waiting for transfers between devices  219 us (68%)
  local copies, waits for them, and re-layouts  31.7 us (10%)
  blocking collectives  28.9 us (9%)
  matrix products  20.4 us (6%)
  between operations  13.2 us (4%)
  other arithmetic  5.58 us (2%)
  starting transfers between devices  3.54 us (1%)
    reduce_scatter x1, waiting for transfers between devices, on_device(): lax.psum_scatter(jnp.dot(attended, out_weight, preferred_element_type=jnp...  85.2 us
    all_gather x1, waiting for transfers between devices, on_device(): lax.all_gather(value_heads, 'blk', axis=1, tiled=True)  72.9 us
    all_gather x1, waiting for transfers between devices, on_device(): lax.all_gather(key_heads, 'blk', axis=1, tiled=True)  51.7 us
    all_to_all x1, blocking collectives, on_device(): lax.all_to_all(key_tokens, 'head', split_axis=1, concat_axis=0, tiled=True)  16.9 us
    all_to_all x1, blocking collectives, on_device(): lax.all_to_all(value_tokens, 'head', split_axis=1, concat_axis=0, tiled=T...  12 us
    sub x1, matrix products, sparse_attend(): weights = jnp.where(mask_full, jnp.exp(scores - peak_value), 0.0)  10.3 us
    all_to_all x1, waiting for transfers between devices, on_device(): lax.all_to_all(query_tokens, 'head', split_axis=1, concat_axis=0, tiled=T...  8.89 us
    gather x1, local copies, waits for them, and re-layouts, on_device(): jnp.take(source_keys, flat_index, axis=1)  8.63 us
  transfers between devices with their start and end apart: 4, of which 4 were waited for; matrix products, arithmetic and copies ran while one was open for 4% of the time, Pallas kernels for 0%

commit v1 on v0

--- a/solution.py
+++ b/solution.py
@@ -35,7 +35,12 @@
 
 def on_device(query_tokens, key_tokens, value_tokens, out_weight, kv_blocks):
     queries, key_rows, value_rows = (
-        lax.all_to_all(query_tokens, "head", split_axis=1, concat_axis=0, tiled=True),
+        jnp.concatenate(
+            lax.all_to_all(
+                jnp.stack(jnp.split(query_tokens, lax.axis_size("head"), axis=1)), "head", 0, 0
+            ),
+            axis=0,
+        ),
         lax.all_to_all(key_tokens, "head", split_axis=1, concat_axis=0, tiled=True),
         lax.all_to_all(value_tokens, "head", split_axis=1, concat_axis=0, tiled=True),
     )

time: 323 us -> 322 us (level)
  waiting for transfers between devices: 219 us -> 209 us
  local copies, waits for them, and re-layouts: 31.7 us -> 41.1 us
    unnamed x6 -> x13, local copies, waits for them, and re-layouts: 0.1 us -> 10 us
    all_gather x1, waiting for transfers between devices: 51.7 us -> 42.7 us  [on_device(): lax.all_gather(key_heads, 'blk', axis=1, tiled=True)]
  transfers between devices with their start and end apart: 4 -> 4, of which waited for: 4 -> 4; matrix products, arithmetic and copies ran while one was open for 4% -> 7% of each run, Pallas kernels for 0% -> 0%
where the time goes in v1:
time: 322 us; the launch traced here: 321 us
  waiting for transfers between devices  209 us (65%)
  local copies, waits for them, and re-layouts  41.1 us (13%)
  blocking collectives  28.9 us (9%)
  matrix products  19.8 us (6%)
  between operations  13.2 us (4%)
  other arithmetic  5.58 us (2%)
  starting transfers between devices  3.54 us (1%)
    reduce_scatter x1, waiting for transfers between devices, on_device(): lax.psum_scatter(jnp.dot(attended, out_weight, preferred_element_type=jnp...  85.2 us
    all_gather x1, waiting for transfers between devices, on_device(): lax.all_gather(value_heads, 'blk', axis=1, tiled=True)  72.3 us
    all_gather x1, waiting for transfers between devices, on_device(): lax.all_gather(key_heads, 'blk', axis=1, tiled=True)  42.7 us
    all_to_all x1, blocking collectives, on_device(): lax.all_to_all(key_tokens, 'head', split_axis=1, concat_axis=0, tiled=True)  16.9 us
    all_to_all x1, blocking collectives, on_device(): lax.all_to_all(value_tokens, 'head', split_axis=1, concat_axis=0, tiled=T...  12 us
    unnamed x13, local copies, waits for them, and re-layouts  10 us
    sub x1, matrix products, sparse_attend(): weights = jnp.where(mask_full, jnp.exp(scores - peak_value), 0.0)  9.97 us
    all_to_all x1, waiting for transfers between devices, on_device(): lax.all_to_all(jnp.stack(jnp.split(query_tokens, lax.axis_size('head'), a...  8.89 us
  transfers between devices with their start and end apart: 4, of which 4 were waited for; matrix products, arithmetic and copies ran while one was open for 7% of the time, Pallas kernels for 0%

profile of v1, /device:TPU:32, one launch (start us, length us, event | category | flops | bytes accessed | tf_op | source)
XLA Modules:
  0.0 321.5 jit_solution(5286598714474629961)
XLA Ops:
  6.5 0.0 copy-start
  6.5 0.0 copy-start.1
  6.5 0.0 all-gather.3.cloned.1.call-start
  6.5 1.2 copy.36
  7.7 16.9 %all_to_all.37 = bf16[64,8,384]{2,0,1:T(8,128)(2,1)S(1)} all-to-all(bf16[64,8,384]{2,0,1:T(8,128)(2,1)S(1)} %bitcast.64), channel_id=1, replica_groups=mesh['blk'=32,'head'=8] {'head'}, dimensions={1} | all-to-all | bytes 786432 | tf_op jit(solution)/shard_map/all_to_all | solution.py:44
  24.7 0.1 reshape.46
  24.8 0.8 copy.23
  25.6 0.0 all-gather.3.cloned.1.call-update
  25.6 0.0 all-gather.5.cloned.1.call-start
  25.6 1.0 copy.35
  26.7 12.0 %all_to_all.38 = bf16[64,8,384]{2,0,1:T(8,128)(2,1)S(1)} all-to-all(bf16[64,8,384]{2,0,1:T(8,128)(2,1)S(1)} %bitcast.65), channel_id=1, replica_groups=mesh['blk'=32,'head'=8] {'head'}, dimensions={1} | all-to-all | bytes 786432 | tf_op jit(solution)/shard_map/all_to_all | solution.py:45
  38.7 0.1 reshape.50
  38.8 0.8 copy.26
  39.7 0.0 all-gather.5.cloned.1.call-update
  39.7 1.4 bitcast_dynamic-update-slice_fusion.7
  41.1 1.4 bitcast_dynamic-update-slice_fusion.6
  42.5 1.4 bitcast_dynamic-update-slice_fusion.5
  43.9 1.4 bitcast_dynamic-update-slice_fusion.4
  45.4 1.4 bitcast_dynamic-update-slice_fusion.3
  46.8 1.4 bitcast_dynamic-update-slice_fusion.2
  48.2 1.4 bitcast_dynamic-update-slice_fusion.1
  49.6 1.4 bitcast_dynamic-update-slice_fusion
  51.0 3.5 %all-to-all-start = ((bf16[8,64,384]{2,1,0:T(8,128)(2,1)}), bf16[8,64,384]{2,1,0:T(8,128)(2,1)S(1)}, u32[]{:S(2)}, u32[]{:S(2)}) async-start(bf16[8,64,384]{2,1,0:T(8,128)(2,1)} %bitcast_dynamic-update-slice_fusion), calls=%async_computation | async-start | bytes 786432 | tf_op jit(solution)/shard_map/all_to_all | solution.py:39
  54.5 0.0 reduce-scatter.2.cloned.1.call-start
  54.5 0.0 copy-done.1
  54.6 0.1 reshape.48
  54.7 0.1 broadcast_bitcast_fusion
  54.8 8.9 %all-to-all-done = bf16[8,64,384]{2,1,0:T(8,128)(2,1)S(1)} async-done(((bf16[8,64,384]{2,1,0:T(8,128)(2,1)}), bf16[8,64,384]{2,1,0:T(8,128)(2,1)S(1)}, u32[]{:S(2)}, u32[]{:S(2)}) %all-to-all-start) | async-done | bytes 393248 | tf_op jit(solution)/shard_map/all_to_all | solution.py:39
  63.7 0.1 reshape_reshape.3
  63.8 0.1 copy.21
  63.9 42.7 %all-gather.3.cloned.1.call-done = bf16[3,16384,128]{2,1,0:T(8,128)(2,1)} async-done(((bf16[3,512,128]{2,1,0:T(8,128)(2,1)}), bf16[3,16384,128]{2,1,0:T(8,128)(2,1)}) %all-gather.3.cloned.1.call-update) | async-done | bytes 12582928 | tf_op jit(solution)/shard_map/all_gather | solution.py:60
  106.6 8.6 %gather_fusion = bf16[64,3,128,128]{3,2,1,0:T(8,128)(2,1)} fusion(bf16[3,128,128,128]{3,2,1,0:T(8,128)(2,1)} %bitcast.57, s32[1024]{0:T(1024)S(1)} %pad_clamp_fusion), kind=kCustom, calls=%fused_computation.clone | custom fusion | bytes 12583168 | tf_op jit(solution)/shard_map/jit(_take)/gather | solution.py:67
  115.2 72.3 %all-gather.5.cloned.1.call-done = bf16[3,16384,128]{2,1,0:T(8,128)(2,1)} async-done(((bf16[3,512,128]{2,1,0:T(8,128)(2,1)}), bf16[3,16384,128]{2,1,0:T(8,128)(2,1)}) %all-gather.5.cloned.1.call-update) | async-done | bytes 12582928 | tf_op jit(solution)/shard_map/all_gather | solution.py:61
  187.5 8.5 %gather_fusion.1 = bf16[64,3,128,128]{3,2,1,0:T(8,128)(2,1)} fusion(bf16[3,128,128,128]{3,2,1,0:T(8,128)(2,1)} %bitcast.58, s32[1024]{0:T(1024)S(1)} %pad_clamp_fusion), kind=kCustom, calls=%fused_computation.1.clone | custom fusion | bytes 12583168 | tf_op jit(solution)/shard_map/jit(_take)/gather | solution.py:70
  196.1 5.5 %select_bitcast_fusion.1 = (bf16[3,64,128,128]{3,2,0,1:T(8,128)(2,1)S(1)}, bf16[3,64,128,128]{3,2,0,1:T(8,128)(2,1)S(1)}) fusion(bf16[64,3,128,128]{3,2,1,0:T(8,128)(2,1)} %gather_fusion, pred[64]{0:T(512)(128)(4,1)S(1)} %compare_and_fusion, bf16[64,3,128,128]{3,2,1,0:T(8,128)(2,1)} %gather_fusion.1), kind=kLoop, calls=%fused_computation.8 | loop fusion | flops 6291456 | bytes 25165888 | tf_op jit(solution)/shard_map/jit(_take)/select_n | solution.py:67
  201.6 4.0 %copy.24 = bf16[3,64,128,128]{3,2,1,0:T(8,128)(2,1)} copy(bf16[3,64,128,128]{3,2,0,1:T(8,128)(2,1)S(1)} %get-tuple-element.6) | data formatting | bytes 12582912 | tf_op jit(solution)/shard_map/jit(_take)/select_n | solution.py:67
  205.6 4.0 %copy.27 = bf16[3,64,128,128]{3,2,1,0:T(8,128)(2,1)} copy(bf16[3,64,128,128]{3,2,0,1:T(8,128)(2,1)S(1)} %get-tuple-element.7) | data formatting | bytes 12582912 | tf_op jit(solution)/shard_map/jit(_take)/select_n | solution.py:70
  209.7 10.0 %fusion.20 = (f32[3,4,128]{2,1,0:T(4,128)S(1)}, bf16[3,4,128,2048]{3,2,1,0:T(8,128)(2,1)}) fusion(pred[4,2048]{1,0:T(4,128)(4,1)S(1)} %bitcast.71, bf16[3,4,128,128]{3,2,1,0:T(8,128)(2,1)S(1)} %bitcast.66, bf16[3,4,2048,128]{3,2,1,0:T(8,128)(2,1)} %bitcast.55), kind=kOutput, calls=%fused_computation.37 | convolution fusion | flops 1632634880 | bytes 12990464 | tf_op jit(solution)/shard_map/sub | solution.py:25
  219.6 6.4 %fusion.13 = bf16[3,4,128,128]{3,2,1,0:T(8,128)(2,1)S(1)} fusion(bf16[3,4,2048,128]{3,2,1,0:T(8,128)(2,1)} %bitcast.56, bf16[3,4,128,2048]{3,2,1,0:T(8,128)(2,1)} %get-tuple-element.9, f32[3,4,128]{2,1,0:T(4,128)S(1)} %get-tuple-element.8), kind=kOutput, calls=%fused_computation.16 | convolution fusion | flops 805699584 | bytes 12982272 | tf_op jit(solution)/shard_map/hbqk,hbkd->hbqd/dot_general | solution.py:27
  226.0 0.2 copy.28
  226.2 0.0 copy-done
  226.2 3.5 %convolution_convert_fusion = bf16[512,3072]{1,0:T(8,128)(2,1)} fusion(bf16[512,384]{0,1:T(8,128)(2,1)S(1)} %bitcast.70, bf16[384,3072]{1,0:T(8,128)(2,1)S(1)} %copy-done), kind=kOutput, calls=%fused_computation.14 | convolution fusion | flops 1209532416 | bytes 5898240 | tf_op jit(solution)/shard_map/dot_general | solution.py:81
  229.7 0.0 reduce-scatter.2.cloned.1.call-update
  229.7 85.2 %reduce-scatter.2.cloned.1.call-done = bf16[64,3072]{1,0:T(8,128)(2,1)} async-done(((bf16[512,3072]{1,0:T(8,128)(2,1)}), bf16[64,3072]{1,0:T(8,128)(2,1)}) %reduce-scatter.2.cloned.1.call-update) | async-done | bytes 393232 | tf_op jit(solution)/shard_map/reduce_scatter | solution.py:80
  (6 shorter events, 0.0 us)
Async XLA Ops:
  6.5 219.7 %copy-start = (bf16[384,3072]{1,0:T(8,128)(2,1)S(1)}, bf16[384,3072]{1,0:T(8,128)(2,1)}, u32[]{:S(2)}) copy-start(bf16[384,3072]{1,0:T(8,128)(2,1)} %param.10) | copy-start | bytes 7077892
  6.5 48.0 %copy-start.1 = (s32[4,16]{1,0:T(4,128)S(1)}, s32[4,16]{1,0:T(4,128)}, u32[]{:S(2)}) copy-start(s32[4,16]{1,0:T(4,128)} %param.11) | copy-start | bytes 772
  6.5 100.1 %all-gather.3.cloned.1.call-start = ((), (), s32[]{:S(2)}) async-start(), calls=%async_computation.4 | async-start | bytes 12976128 | tf_op jit(solution)/shard_map/all_gather | solution.py:60
  25.6 161.9 %all-gather.5.cloned.1.call-start = ((), (), s32[]{:S(2)}) async-start(), calls=%async_computation.5 | async-start | bytes 12976128 | tf_op jit(solution)/shard_map/all_gather | solution.py:61
  51.0 12.6 %all-to-all-start = ((bf16[8,64,384]{2,1,0:T(8,128)(2,1)}), bf16[8,64,384]{2,1,0:T(8,128)(2,1)S(1)}, u32[]{:S(2)}, u32[]{:S(2)}) async-start(bf16[8,64,384]{2,1,0:T(8,128)(2,1)} %bitcast_dynamic-update-slice_fusion), calls=%async_computation | async-start | bytes 786432 | tf_op jit(solution)/shard_map/all_to_all | solution.py:39
  54.5 260.5 %reduce-scatter.2.cloned.1.call-start = ((), (), s32[]{:S(2)}) async-start(), calls=%async_computation.6 | async-start | bytes 3538944 | tf_op jit(solution)/shard_map/reduce_scatter | solution.py:80
Sparse Core Ops, SparseCore 0:
  25.7 80.8 all-gather.2
  108.5 79.0 all-gather.4
  229.8 85.0 reduce-scatter.1
